TPU v7x, 32 devices: a whole 2x2x4 slice. The times are simulated.
32 devices in a mesh: groups: 2 (over y), tiles: 4 (over z), section: 4 (over x, core).
Axes of the slice: x: 2, y: 2, z: 4, core: 2. Of those that a mesh axis runs over, the one named last changes fastest.
Arguments:
- latents: float32 [4, 192, 8, 128], P('groups', None, 'tiles'), parts along dimension 0, may hold values from -6 to 6
- conv_weight: float32 [4, 27, 192, 192], P('section'), may hold values from -0.078125 to 0.078125
- gain: float32 [4, 192], P('section'), may hold values from 0.1 to 1.9
Outputs:
- decoded: float32 [4, 192, 8, 128], P('groups', 'section', 'tiles'), parts along dimension 0
There are 2 independent parts, one for each index of `groups`. A program takes and returns all parts, laid end to end along the dimension named above; an argument that names none is the same for every part. Nothing has to cross between parts.
All inputs are finite; a program needn't handle non-finite values.
Results may differ from a plain program's by a relative error of at most 0.00013.
Values sent between devices are 32-bit elements; how exact they have to be, the bound alone decides.
No kernel may reach another device: no remote copies, remote signals or barrier semaphores. Data moves between devices by JAX's collectives and lax.ppermute only.
A program may use at most 64 MiB of HBM per device.

v0:
```python
import jax
import jax.numpy as jnp
from jax import lax
from jax.sharding import PartitionSpec as P

EPSILON = 1e-06


def extended(block, sides, width):
    for axis, dim in sides:
        count = lax.axis_size(axis)
        forward = [(i, i + 1) for i in range(count - 1)]
        backward = [(target, source) for source, target in forward]
        low = lax.ppermute(
            lax.slice_in_dim(block, block.shape[dim] - width, None, axis=dim), axis, forward
        )
        high = lax.ppermute(lax.slice_in_dim(block, 0, width, axis=dim), axis, backward)
        block = jnp.concatenate([low, block, high], axis=dim)
    return block


def from_behind(value, axis, by):
    peers = lax.axis_size(axis)
    pairs = [(i, i + by) for i in range(peers) if 0 <= i + by < peers]
    return lax.ppermute(value, axis, pairs)


def broadcast(value, axis, source):
    kept = jnp.where(lax.axis_index(axis) == source, value, 0).astype(value.dtype)
    return lax.psum(kept, axis)


def normalize(values, gain_row):
    meansq = jnp.mean(values * values, axis=1, keepdims=True)
    scaled = values * lax.rsqrt(meansq + EPSILON) * gain_row[None, :, None, None]
    return jax.nn.silu(scaled)


def add_rim(normed):
    return extended(normed, (("tiles", 2),), 1)


def convolve(padded, kernel, block_len, rows_here, col_count):
    summed = jnp.zeros((block_len, kernel.shape[1], rows_here, col_count), jnp.float32)
    for time_off in range(3):
        for row_off in range(3):
            for col_off in range(3):
                window = padded[
                    time_off : time_off + block_len,
                    :,
                    row_off : row_off + rows_here,
                    col_off : col_off + col_count,
                ]
                summed = summed + jnp.einsum(
                    "oi,tirw->torw",
                    kernel[time_off * 9 + row_off * 3 + col_off],
                    window,
                    precision=lax.Precision.HIGHEST,
                )
    return summed


def by_layers(latents, conv_weight, gain):
    kernel = conv_weight[0]
    gain_row = gain[0]
    frame_count, channels, rows_here, col_count = latents.shape
    layer_count = lax.axis_size("section")
    position = lax.axis_index("section")
    block_count = frame_count // frame_count
    step_count = block_count + layer_count - 1
    initial = jnp.zeros((frame_count, channels, rows_here, col_count), jnp.float32)
    memory_init = jnp.zeros((2, channels, rows_here + 2, col_count), jnp.float32)
    results_init = jnp.zeros_like(latents)

    def compute(operand):
        return convolve(operand, kernel, frame_count, rows_here, col_count)

    def skipped(operand):
        return jnp.zeros((frame_count, channels, rows_here, col_count), jnp.float32)

    def advance(step_now, loop_state):
        passing, memory, results = loop_state
        incoming = from_behind(passing, "section", 1)
        block_index = step_now - position
        active = (block_index >= 0) & (block_index < block_count)
        source = jnp.where(position == 0, latents, incoming)
        normed = normalize(source, gain_row)
        with_rim = add_rim(normed)
        joined = jnp.concatenate([memory, with_rim], axis=0)
        padded = jnp.pad(joined, ((0, 0), (0, 0), (0, 0), (1, 1)))
        branch = lax.cond(active, compute, skipped, padded)
        output = source + branch
        memory = jnp.where(active, joined[-2:], memory)
        store_now = active & (position == layer_count - 1)
        results = jnp.where(store_now, output, results)
        return (output, memory, results)

    final_state = lax.fori_loop(0, step_count, advance, (initial, memory_init, results_init))
    gathered = broadcast(final_state[2], "section", layer_count - 1)
    share = channels // layer_count
    return lax.dynamic_slice_in_dim(gathered, position * share, share, 1)


def local(latents, conv_weight, gain):
    return by_layers(latents, conv_weight, gain)


def solution(mesh):
    return jax.shard_map(
        local,
        mesh=mesh,
        in_specs=(
            P("groups", None, "tiles", None),
            P("section", None, None, None),
            P("section", None),
        ),
        out_specs=P("groups", "section", "tiles", None),
        check_vma=False,
    )
```

profile of v0, /device:TPU:0, one launch (start us, length us, event | category | flops | bytes accessed | tf_op | source)
XLA Modules:
  0.0 192.6 jit_solution(15802440383919716907)
XLA Ops:
  6.5 1.0 copy.4
  7.6 99.6 %while.20 = (s32[]{:T(128)}, f32[2,192,2,128]{3,1,2,0:T(8,128)S(1)}, f32[2,192,4,128]{3,1,2,0:T(8,128)S(1)}, f32[2,192,2,128]{3,1,2,0:T(8,128)S(1)}, pred[]{:T(5...) while((s32[]{:T(128)}, ...), condition=%wide.region_4.5_spmd.clone, body=%wide.region_0.4_spmd.clone.sunk | while | flops 6121095680 | bytes 99492952 | solution.py:98
  7.6 2.4 %collective-permute-start = (f32[2,192,2,128]{3,1,2,0:T(8,128)S(1)}, f32[2,192,2,128]{3,1,2,0:T(8,128)S(1)}, u32[]{:S(2)}, u32[]{:S(2)}) collective-permute-start(f32[2,192,2,128]{3,1,2,0:T(8,128)S(1)} %broadcast_select_fusion.6), channel_id=1, source_target_pairs={{0,1},{1,2},{2,3},{4,5},{5,6},{6,7},{8,9},{9,10},{10,11},{12,13},{... | collective-permute-start | bytes 1179656 | tf_op jit(solution)/shard_map/while/body/eval_jaxpr/ppermute | solution.py:25
  10.0 1.3 collective-permute-done
  11.4 0.9 divide_multiply_fusion.2
  12.3 1.3 collective-permute-start.1
  13.6 4.9 %collective-permute-start.2 = (f32[2,192,1,128]{3,1,2,0:T(8,128)S(1)}, f32[2,192,1,128]{3,1,2,0:T(8,128)S(1)}, u32[]{:S(2)}, u32[]{:S(2)}) collective-permute-start(f32[2,192,1,128]{3,1,2,0:T(8,128)S(1)} %get-tuple-element.376), channel_id=1, source_target_pairs={{0,4},{4,8},{8,12},{1,5},{5,9},{9,13},{2,6},{6,10},{10,14},{3,7},{... | collective-permute-start | bytes 589832 | tf_op jit(solution)/shard_map/while/body/eval_jaxpr/ppermute | solution.py:14
  18.6 1.7 collective-permute-done.1
  20.3 1.5 collective-permute-done.2
  22.1 19.5 %conditional.3 = (f32[2,192,2,128]{3,1,2,0:T(8,128)S(1)}) conditional(s32[]{:T(128)} %convert_element_type.22, () %tuple.63, (f32[4,192,4,128]{3,1,2,0:T(8,128)S(1)}, f32[27,192,192]{2,1,0:T(8,128)}) %tuple.64), branch_computations={%region_2.2_spmd, %region_3.3_spmd} | conditional | flops 6117851136 | bytes 84541480 | solution.py:91
  22.1 1.6 fusion.46
  23.8 1.6 convolution_add_fusion.10
  25.4 1.6 convolution_add_fusion.9
  27.5 0.7 fusion.7
  28.1 0.6 convolution_add_fusion.7
  29.3 0.7 fusion.8
  31.2 0.7 fusion.9
  31.8 0.6 convolution_add_fusion.3
  33.0 0.7 fusion.10
  33.7 0.6 convolution_add_fusion.1
  34.9 0.7 fusion.12
  35.5 0.6 fusion
  38.0 0.6 fusion.3
  39.2 0.6 fusion.4
  41.9 1.3 collective-permute-start
  43.2 1.3 collective-permute-done
  44.6 0.9 divide_multiply_fusion.2
  45.5 1.3 collective-permute-start.1
  46.8 5.0 %collective-permute-start.2 = (f32[2,192,1,128]{3,1,2,0:T(8,128)S(1)}, f32[2,192,1,128]{3,1,2,0:T(8,128)S(1)}, u32[]{:S(2)}, u32[]{:S(2)}) collective-permute-start(f32[2,192,1,128]{3,1,2,0:T(8,128)S(1)} %get-tuple-element.376), channel_id=1, source_target_pairs={{0,4},{4,8},{8,12},{1,5},{5,9},{9,13},{2,6},{6,10},{10,14},{3,7},{... | collective-permute-start | bytes 589832 | tf_op jit(solution)/shard_map/while/body/eval_jaxpr/ppermute | solution.py:14
  51.8 3.5 %collective-permute-done.1 = f32[2,192,1,128]{3,1,2,0:T(8,128)S(1)} collective-permute-done((f32[2,192,1,128]{3,1,2,0:T(8,128)S(1)}, f32[2,192,1,128]{3,1,2,0:T(8,128)S(1)}, u32[]{:S(2)}, u32[]{:S(2)}) %collective-permute-start.1) | collective-permute-done | bytes 196640 | tf_op jit(solution)/shard_map/while/body/eval_jaxpr/ppermute | solution.py:17
  55.3 1.2 collective-permute-done.2
  57.2 20.9 %collective-permute-start = (f32[2,192,2,128]{3,1,2,0:T(8,128)S(1)}, f32[2,192,2,128]{3,1,2,0:T(8,128)S(1)}, u32[]{:S(2)}, u32[]{:S(2)}) collective-permute-start(f32[2,192,2,128]{3,1,2,0:T(8,128)S(1)} %broadcast_select_fusion.6), channel_id=1, source_target_pairs={{0,1},{1,2},{2,3},{4,5},{5,6},{6,7},{8,9},{9,10},{10,11},{12,13},{... | collective-permute-start | bytes 1179656 | tf_op jit(solution)/shard_map/while/body/eval_jaxpr/ppermute | solution.py:25
  78.1 1.3 collective-permute-done
  79.5 0.9 divide_multiply_fusion.2
  80.4 1.3 collective-permute-start.1
  81.7 5.0 %collective-permute-start.2 = (f32[2,192,1,128]{3,1,2,0:T(8,128)S(1)}, f32[2,192,1,128]{3,1,2,0:T(8,128)S(1)}, u32[]{:S(2)}, u32[]{:S(2)}) collective-permute-start(f32[2,192,1,128]{3,1,2,0:T(8,128)S(1)} %get-tuple-element.376), channel_id=1, source_target_pairs={{0,4},{4,8},{8,12},{1,5},{5,9},{9,13},{2,6},{6,10},{10,14},{3,7},{... | collective-permute-start | bytes 589832 | tf_op jit(solution)/shard_map/while/body/eval_jaxpr/ppermute | solution.py:14
  86.7 1.7 collective-permute-done.1
  88.4 1.5 collective-permute-done.2
  90.5 4.5 %collective-permute-start = (f32[2,192,2,128]{3,1,2,0:T(8,128)S(1)}, f32[2,192,2,128]{3,1,2,0:T(8,128)S(1)}, u32[]{:S(2)}, u32[]{:S(2)}) collective-permute-start(f32[2,192,2,128]{3,1,2,0:T(8,128)S(1)} %broadcast_select_fusion.6), channel_id=1, source_target_pairs={{0,1},{1,2},{2,3},{4,5},{5,6},{6,7},{8,9},{9,10},{10,11},{12,13},{... | collective-permute-start | bytes 1179656 | tf_op jit(solution)/shard_map/while/body/eval_jaxpr/ppermute | solution.py:25
  95.0 1.3 collective-permute-done
  96.4 0.9 divide_multiply_fusion.2
  97.3 1.3 collective-permute-start.1
  98.6 4.7 %collective-permute-start.2 = (f32[2,192,1,128]{3,1,2,0:T(8,128)S(1)}, f32[2,192,1,128]{3,1,2,0:T(8,128)S(1)}, u32[]{:S(2)}, u32[]{:S(2)}) collective-permute-start(f32[2,192,1,128]{3,1,2,0:T(8,128)S(1)} %get-tuple-element.376), channel_id=1, source_target_pairs={{0,4},{4,8},{8,12},{1,5},{5,9},{9,13},{2,6},{6,10},{10,14},{3,7},{... | collective-permute-start | bytes 589832 | tf_op jit(solution)/shard_map/while/body/eval_jaxpr/ppermute | solution.py:14
  103.3 1.7 collective-permute-done.1
  105.0 1.5 collective-permute-done.2
  107.1 1.1 copy_select_fusion
  108.3 76.0 %all-reduce.3.cloned.1.call-done = f32[2,192,2,128]{3,2,1,0:T(2,128)} async-done(((f32[2,192,2,128]{3,2,1,0:T(2,128)}), f32[2,192,2,128]{3,2,1,0:T(2,128)}) %all-reduce.3.cloned.1.call-update) | async-done | bytes 393232 | tf_op jit(solution)/shard_map/psum | solution.py:30
  184.2 1.5 constant_dynamic-slice_fusion
  (54 shorter events, 10.4 us)
Async XLA Ops:
  6.5 177.7 %all-reduce.3.cloned.1.call-start = ((), (), s32[]{:S(2)}) async-start(), calls=%async_computation | async-start | bytes 786432 | tf_op jit(solution)/shard_map/psum | solution.py:30
  7.6 3.7 %collective-permute-start = (f32[2,192,2,128]{3,1,2,0:T(8,128)S(1)}, f32[2,192,2,128]{3,1,2,0:T(8,128)S(1)}, u32[]{:S(2)}, u32[]{:S(2)}) collective-permute-start(f32[2,192,2,128]{3,1,2,0:T(8,128)S(1)} %broadcast_select_fusion.6), channel_id=1, source_target_pairs={{0,1},{1,2},{2,3},{4,5},{5,6},{6,7},{8,9},{9,10},{10,11},{12,13},{... | collective-permute-start | bytes 1179656 | tf_op jit(solution)/shard_map/while/body/eval_jaxpr/ppermute | solution.py:25
  12.3 7.9 %collective-permute-start.1 = (f32[2,192,1,128]{3,1,2,0:T(8,128)S(1)}, f32[2,192,1,128]{3,1,2,0:T(8,128)S(1)}, u32[]{:S(2)}, u32[]{:S(2)}) collective-permute-start(f32[2,192,1,128]{3,1,2,0:T(8,128)S(1)} %get-tuple-element.375), channel_id=1, source_target_pairs={{4,0},{8,4},{12,8},{5,1},{9,5},{13,9},{6,2},{10,6},{14,10},{7,3},{... | collective-permute-start | bytes 589832 | tf_op jit(solution)/shard_map/while/body/eval_jaxpr/ppermute | solution.py:17
  13.6 8.1 %collective-permute-start.2 = (f32[2,192,1,128]{3,1,2,0:T(8,128)S(1)}, f32[2,192,1,128]{3,1,2,0:T(8,128)S(1)}, u32[]{:S(2)}, u32[]{:S(2)}) collective-permute-start(f32[2,192,1,128]{3,1,2,0:T(8,128)S(1)} %get-tuple-element.376), channel_id=1, source_target_pairs={{0,4},{4,8},{8,12},{1,5},{5,9},{9,13},{2,6},{6,10},{10,14},{3,7},{... | collective-permute-start | bytes 589832 | tf_op jit(solution)/shard_map/while/body/eval_jaxpr/ppermute | solution.py:14
  22.1 4.8 %copy-start = (f32[27,192,192]{2,1,0:T(8,128)S(1)}, f32[27,192,192]{2,1,0:T(8,128)}, u32[]{:S(2)}) copy-start(f32[27,192,192]{2,1,0:T(8,128)} %get-tuple-element.219) | copy-start | bytes 11943940 | tf_op jit(solution)/shard_map/while/body/eval_jaxpr/cond
  41.9 2.6 %collective-permute-start = (f32[2,192,2,128]{3,1,2,0:T(8,128)S(1)}, f32[2,192,2,128]{3,1,2,0:T(8,128)S(1)}, u32[]{:S(2)}, u32[]{:S(2)}) collective-permute-start(f32[2,192,2,128]{3,1,2,0:T(8,128)S(1)} %broadcast_select_fusion.6), channel_id=1, source_target_pairs={{0,1},{1,2},{2,3},{4,5},{5,6},{6,7},{8,9},{9,10},{10,11},{12,13},{... | collective-permute-start | bytes 1179656 | tf_op jit(solution)/shard_map/while/body/eval_jaxpr/ppermute | solution.py:25
  45.5 9.8 %collective-permute-start.1 = (f32[2,192,1,128]{3,1,2,0:T(8,128)S(1)}, f32[2,192,1,128]{3,1,2,0:T(8,128)S(1)}, u32[]{:S(2)}, u32[]{:S(2)}) collective-permute-start(f32[2,192,1,128]{3,1,2,0:T(8,128)S(1)} %get-tuple-element.375), channel_id=1, source_target_pairs={{4,0},{8,4},{12,8},{5,1},{9,5},{13,9},{6,2},{10,6},{14,10},{7,3},{... | collective-permute-start | bytes 589832 | tf_op jit(solution)/shard_map/while/body/eval_jaxpr/ppermute | solution.py:17
  46.8 9.7 %collective-permute-start.2 = (f32[2,192,1,128]{3,1,2,0:T(8,128)S(1)}, f32[2,192,1,128]{3,1,2,0:T(8,128)S(1)}, u32[]{:S(2)}, u32[]{:S(2)}) collective-permute-start(f32[2,192,1,128]{3,1,2,0:T(8,128)S(1)} %get-tuple-element.376), channel_id=1, source_target_pairs={{0,4},{4,8},{8,12},{1,5},{5,9},{9,13},{2,6},{6,10},{10,14},{3,7},{... | collective-permute-start | bytes 589832 | tf_op jit(solution)/shard_map/while/body/eval_jaxpr/ppermute | solution.py:14
  57.2 22.2 %collective-permute-start = (f32[2,192,2,128]{3,1,2,0:T(8,128)S(1)}, f32[2,192,2,128]{3,1,2,0:T(8,128)S(1)}, u32[]{:S(2)}, u32[]{:S(2)}) collective-permute-start(f32[2,192,2,128]{3,1,2,0:T(8,128)S(1)} %broadcast_select_fusion.6), channel_id=1, source_target_pairs={{0,1},{1,2},{2,3},{4,5},{5,6},{6,7},{8,9},{9,10},{10,11},{12,13},{... | collective-permute-start | bytes 1179656 | tf_op jit(solution)/shard_map/while/body/eval_jaxpr/ppermute | solution.py:25
  80.4 8.0 %collective-permute-start.1 = (f32[2,192,1,128]{3,1,2,0:T(8,128)S(1)}, f32[2,192,1,128]{3,1,2,0:T(8,128)S(1)}, u32[]{:S(2)}, u32[]{:S(2)}) collective-permute-start(f32[2,192,1,128]{3,1,2,0:T(8,128)S(1)} %get-tuple-element.375), channel_id=1, source_target_pairs={{4,0},{8,4},{12,8},{5,1},{9,5},{13,9},{6,2},{10,6},{14,10},{7,3},{... | collective-permute-start | bytes 589832 | tf_op jit(solution)/shard_map/while/body/eval_jaxpr/ppermute | solution.py:17
  81.7 8.2 %collective-permute-start.2 = (f32[2,192,1,128]{3,1,2,0:T(8,128)S(1)}, f32[2,192,1,128]{3,1,2,0:T(8,128)S(1)}, u32[]{:S(2)}, u32[]{:S(2)}) collective-permute-start(f32[2,192,1,128]{3,1,2,0:T(8,128)S(1)} %get-tuple-element.376), channel_id=1, source_target_pairs={{0,4},{4,8},{8,12},{1,5},{5,9},{9,13},{2,6},{6,10},{10,14},{3,7},{... | collective-permute-start | bytes 589832 | tf_op jit(solution)/shard_map/while/body/eval_jaxpr/ppermute | solution.py:14
  90.5 5.8 %collective-permute-start = (f32[2,192,2,128]{3,1,2,0:T(8,128)S(1)}, f32[2,192,2,128]{3,1,2,0:T(8,128)S(1)}, u32[]{:S(2)}, u32[]{:S(2)}) collective-permute-start(f32[2,192,2,128]{3,1,2,0:T(8,128)S(1)} %broadcast_select_fusion.6), channel_id=1, source_target_pairs={{0,1},{1,2},{2,3},{4,5},{5,6},{6,7},{8,9},{9,10},{10,11},{12,13},{... | collective-permute-start | bytes 1179656 | tf_op jit(solution)/shard_map/while/body/eval_jaxpr/ppermute | solution.py:25
  97.3 7.7 %collective-permute-start.1 = (f32[2,192,1,128]{3,1,2,0:T(8,128)S(1)}, f32[2,192,1,128]{3,1,2,0:T(8,128)S(1)}, u32[]{:S(2)}, u32[]{:S(2)}) collective-permute-start(f32[2,192,1,128]{3,1,2,0:T(8,128)S(1)} %get-tuple-element.375), channel_id=1, source_target_pairs={{4,0},{8,4},{12,8},{5,1},{9,5},{13,9},{6,2},{10,6},{14,10},{7,3},{... | collective-permute-start | bytes 589832 | tf_op jit(solution)/shard_map/while/body/eval_jaxpr/ppermute | solution.py:17
  98.6 7.9 %collective-permute-start.2 = (f32[2,192,1,128]{3,1,2,0:T(8,128)S(1)}, f32[2,192,1,128]{3,1,2,0:T(8,128)S(1)}, u32[]{:S(2)}, u32[]{:S(2)}) collective-permute-start(f32[2,192,1,128]{3,1,2,0:T(8,128)S(1)} %get-tuple-element.376), channel_id=1, source_target_pairs={{0,4},{4,8},{8,12},{1,5},{5,9},{9,13},{2,6},{6,10},{10,14},{3,7},{... | collective-permute-start | bytes 589832 | tf_op jit(solution)/shard_map/while/body/eval_jaxpr/ppermute | solution.py:14
Sparse Core Ops, SparseCore 0:
  108.4 75.7 all-reduce.2
where the time goes:
time: 193 us
  waiting for transfers between devices  95.3 us (49%)
  starting transfers between devices  54 us (28%)
  matrix products  19.3 us (10%)
  between operations  13.4 us (7%)
  other arithmetic  7.2 us (4%)
  local copies, waits for them, and re-layouts  2.76 us (1%)
    psum x1, waiting for transfers between devices, broadcast(): return lax.psum(kept, axis)  76 us
    ppermute x4, starting transfers between devices, from_behind(): return lax.ppermute(value, axis, pairs)  29.1 us
    ppermute x4, starting transfers between devices, extended(): lax.ppermute(lax.slice_in_dim(block, block.shape[dim] - width, None, axis...  19.7 us
    dot_general x27, matrix products, convolve(): jnp.einsum('oi,tirw->torw', kernel[time_off * 9 + row_off * 3 + col_off],...  19.3 us
    ppermute x4, waiting for transfers between devices, extended(): lax.ppermute(lax.slice_in_dim(block, 0, width, axis=dim), axis, backward)  8.53 us
    ppermute x4, waiting for transfers between devices, extended(): lax.ppermute(lax.slice_in_dim(block, block.shape[dim] - width, None, axis...  5.56 us
    ppermute x4, waiting for transfers between devices, from_behind(): return lax.ppermute(value, axis, pairs)  5.23 us
    ppermute x4, starting transfers between devices, extended(): lax.ppermute(lax.slice_in_dim(block, 0, width, axis=dim), axis, backward)  5.17 us
  transfers between devices with their start and end apart: 13, of which 13 were waited for; matrix products, arithmetic and copies ran while one was open for 0% of the time, Pallas kernels for 0%

commit v1 on v0

--- a/solution.py
+++ b/solution.py
@@ -4,6 +4,12 @@
 from jax.sharding import PartitionSpec as P
 
 EPSILON = 1e-06
+
+
+def gather_and_add(array, mesh_axis):
+    parts = lax.all_gather(array, mesh_axis, axis=0, tiled=False)
+    result = parts.sum(axis=0)
+    return result
 
 
 def extended(block, sides, width):
@@ -27,7 +33,7 @@
 
 def broadcast(value, axis, source):
     kept = jnp.where(lax.axis_index(axis) == source, value, 0).astype(value.dtype)
-    return lax.psum(kept, axis)
+    return gather_and_add(kept, axis)
 
 
 def normalize(values, gain_row):

time: 193 us -> 180 us (0.933)
  waiting for transfers between devices: 95.3 us -> 81.9 us
    psum x1 -> x0, waiting for transfers between devices: 76 us -> none  [broadcast(): return lax.psum(kept, axis)]
    all_gather x0 -> x1, waiting for transfers between devices: none -> 62.6 us  [gather_and_add(): parts = lax.all_gather(array, mesh_axis, axis=0, tiled=False)]
where the time goes in v1:
time: 180 us; the launch traced here: 179 us
  waiting for transfers between devices  81.9 us (46%)
  starting transfers between devices  53.9 us (30%)
  matrix products  19.1 us (11%)
  between operations  13.4 us (7%)
  other arithmetic  8.44 us (5%)
  local copies, waits for them, and re-layouts  1.93 us (1%)
    all_gather x1, waiting for transfers between devices, gather_and_add(): parts = lax.all_gather(array, mesh_axis, axis=0, tiled=False)  62.6 us
    ppermute x4, starting transfers between devices, from_behind(): return lax.ppermute(value, axis, pairs)  29 us
    ppermute x4, starting transfers between devices, extended(): lax.ppermute(lax.slice_in_dim(block, block.shape[dim] - width, None, axis...  19.7 us
    dot_general x27, matrix products, convolve(): jnp.einsum('oi,tirw->torw', kernel[time_off * 9 + row_off * 3 + col_off],...  19.1 us
    ppermute x4, waiting for transfers between devices, extended(): lax.ppermute(lax.slice_in_dim(block, 0, width, axis=dim), axis, backward)  8.53 us
    ppermute x4, waiting for transfers between devices, extended(): lax.ppermute(lax.slice_in_dim(block, block.shape[dim] - width, None, axis...  5.56 us
    ppermute x4, waiting for transfers between devices, from_behind(): return lax.ppermute(value, axis, pairs)  5.23 us
    ppermute x4, starting transfers between devices, extended(): lax.ppermute(lax.slice_in_dim(block, 0, width, axis=dim), axis, backward)  5.17 us
  transfers between devices with their start and end apart: 13, of which 13 were waited for; matrix products, arithmetic and copies ran while one was open for 0% of the time, Pallas kernels for 0%

profile of v1, /device:TPU:0, one launch (start us, length us, event | category | flops | bytes accessed | tf_op | source)
XLA Modules:
  0.0 179.4 jit_solution(15946517350453860792)
XLA Ops:
  6.5 1.0 copy.5
  7.6 99.4 %while.20 = (s32[]{:T(128)}, f32[2,192,2,128]{3,1,2,0:T(8,128)S(1)}, f32[2,192,4,128]{3,1,2,0:T(8,128)S(1)}, f32[2,192,2,128]{3,1,2,0:T(8,128)S(1)}, pred[]{:T(5...) while((s32[]{:T(128)}, ...), condition=%wide.region_4.5_spmd.clone, body=%wide.region_0.4_spmd.clone.sunk | while | flops 6121095680 | bytes 99492952 | solution.py:104
  7.6 2.4 %collective-permute-start = (f32[2,192,2,128]{3,1,2,0:T(8,128)S(1)}, f32[2,192,2,128]{3,1,2,0:T(8,128)S(1)}, u32[]{:S(2)}, u32[]{:S(2)}) collective-permute-start(f32[2,192,2,128]{3,1,2,0:T(8,128)S(1)} %broadcast_select_fusion.7), channel_id=1, source_target_pairs={{0,1},{1,2},{2,3},{4,5},{5,6},{6,7},{8,9},{9,10},{10,11},{12,13},{... | collective-permute-start | bytes 1179656 | tf_op jit(solution)/shard_map/while/body/eval_jaxpr/ppermute | solution.py:31
  10.0 1.3 collective-permute-done
  11.4 0.9 divide_multiply_fusion.2
  12.3 1.3 collective-permute-start.1
  13.6 4.9 %collective-permute-start.2 = (f32[2,192,1,128]{3,1,2,0:T(8,128)S(1)}, f32[2,192,1,128]{3,1,2,0:T(8,128)S(1)}, u32[]{:S(2)}, u32[]{:S(2)}) collective-permute-start(f32[2,192,1,128]{3,1,2,0:T(8,128)S(1)} %get-tuple-element.386), channel_id=1, source_target_pairs={{0,4},{4,8},{8,12},{1,5},{5,9},{9,13},{2,6},{6,10},{10,14},{3,7},{... | collective-permute-start | bytes 589832 | tf_op jit(solution)/shard_map/while/body/eval_jaxpr/ppermute | solution.py:20
  18.6 1.7 collective-permute-done.1
  20.3 1.5 collective-permute-done.2
  22.1 19.4 %conditional.3 = (f32[2,192,2,128]{3,1,2,0:T(8,128)S(1)}) conditional(s32[]{:T(128)} %convert_element_type.22, () %tuple.64, (f32[4,192,4,128]{3,1,2,0:T(8,128)S(1)}, f32[27,192,192]{2,1,0:T(8,128)}) %tuple.65), branch_computations={%region_2.2_spmd, %region_3.3_spmd} | conditional | flops 6117851136 | bytes 84541480 | solution.py:97
  22.2 1.6 fusion.46
  23.8 1.6 convolution_add_fusion.10
  25.4 1.6 convolution_add_fusion.9
  27.5 0.7 fusion.7
  29.3 0.7 fusion.8
  31.1 0.7 fusion.9
  33.0 0.7 fusion.10
  34.8 0.6 fusion.12
  35.4 0.6 fusion
  36.1 0.6 fusion.1
  37.2 0.6 fusion.2
  37.9 0.6 fusion.3
  40.9 0.6 fusion.6
  41.8 1.3 collective-permute-start
  43.1 1.3 collective-permute-done
  44.5 0.9 divide_multiply_fusion.2
  45.4 1.3 collective-permute-start.1
  46.7 5.0 %collective-permute-start.2 = (f32[2,192,1,128]{3,1,2,0:T(8,128)S(1)}, f32[2,192,1,128]{3,1,2,0:T(8,128)S(1)}, u32[]{:S(2)}, u32[]{:S(2)}) collective-permute-start(f32[2,192,1,128]{3,1,2,0:T(8,128)S(1)} %get-tuple-element.386), channel_id=1, source_target_pairs={{0,4},{4,8},{8,12},{1,5},{5,9},{9,13},{2,6},{6,10},{10,14},{3,7},{... | collective-permute-start | bytes 589832 | tf_op jit(solution)/shard_map/while/body/eval_jaxpr/ppermute | solution.py:20
  51.7 3.5 %collective-permute-done.1 = f32[2,192,1,128]{3,1,2,0:T(8,128)S(1)} collective-permute-done((f32[2,192,1,128]{3,1,2,0:T(8,128)S(1)}, f32[2,192,1,128]{3,1,2,0:T(8,128)S(1)}, u32[]{:S(2)}, u32[]{:S(2)}) %collective-permute-start.1) | collective-permute-done | bytes 196640 | tf_op jit(solution)/shard_map/while/body/eval_jaxpr/ppermute | solution.py:23
  55.2 1.2 collective-permute-done.2
  57.1 20.8 %collective-permute-start = (f32[2,192,2,128]{3,1,2,0:T(8,128)S(1)}, f32[2,192,2,128]{3,1,2,0:T(8,128)S(1)}, u32[]{:S(2)}, u32[]{:S(2)}) collective-permute-start(f32[2,192,2,128]{3,1,2,0:T(8,128)S(1)} %broadcast_select_fusion.7), channel_id=1, source_target_pairs={{0,1},{1,2},{2,3},{4,5},{5,6},{6,7},{8,9},{9,10},{10,11},{12,13},{... | collective-permute-start | bytes 1179656 | tf_op jit(solution)/shard_map/while/body/eval_jaxpr/ppermute | solution.py:31
  77.9 1.3 collective-permute-done
  79.3 0.9 divide_multiply_fusion.2
  80.2 1.3 collective-permute-start.1
  81.5 5.0 %collective-permute-start.2 = (f32[2,192,1,128]{3,1,2,0:T(8,128)S(1)}, f32[2,192,1,128]{3,1,2,0:T(8,128)S(1)}, u32[]{:S(2)}, u32[]{:S(2)}) collective-permute-start(f32[2,192,1,128]{3,1,2,0:T(8,128)S(1)} %get-tuple-element.386), channel_id=1, source_target_pairs={{0,4},{4,8},{8,12},{1,5},{5,9},{9,13},{2,6},{6,10},{10,14},{3,7},{... | collective-permute-start | bytes 589832 | tf_op jit(solution)/shard_map/while/body/eval_jaxpr/ppermute | solution.py:20
  86.5 1.7 collective-permute-done.1
  88.2 1.5 collective-permute-done.2
  90.4 4.5 %collective-permute-start = (f32[2,192,2,128]{3,1,2,0:T(8,128)S(1)}, f32[2,192,2,128]{3,1,2,0:T(8,128)S(1)}, u32[]{:S(2)}, u32[]{:S(2)}) collective-permute-start(f32[2,192,2,128]{3,1,2,0:T(8,128)S(1)} %broadcast_select_fusion.7), channel_id=1, source_target_pairs={{0,1},{1,2},{2,3},{4,5},{5,6},{6,7},{8,9},{9,10},{10,11},{12,13},{... | collective-permute-start | bytes 1179656 | tf_op jit(solution)/shard_map/while/body/eval_jaxpr/ppermute | solution.py:31
  94.8 1.3 collective-permute-done
  96.2 0.9 divide_multiply_fusion.2
  97.1 1.3 collective-permute-start.1
  98.4 4.7 %collective-permute-start.2 = (f32[2,192,1,128]{3,1,2,0:T(8,128)S(1)}, f32[2,192,1,128]{3,1,2,0:T(8,128)S(1)}, u32[]{:S(2)}, u32[]{:S(2)}) collective-permute-start(f32[2,192,1,128]{3,1,2,0:T(8,128)S(1)} %get-tuple-element.386), channel_id=1, source_target_pairs={{0,4},{4,8},{8,12},{1,5},{5,9},{9,13},{2,6},{6,10},{10,14},{3,7},{... | collective-permute-start | bytes 589832 | tf_op jit(solution)/shard_map/while/body/eval_jaxpr/ppermute | solution.py:20
  103.2 1.7 collective-permute-done.1
  104.8 1.5 collective-permute-done.2
  107.0 0.8 broadcast_select_fusion.3
  107.8 62.6 %all-gather.3.cloned.1.call-done = f32[8,192,2,128]{3,1,2,0:T(8,128)} async-done(((f32[2,192,2,128]{3,1,2,0:T(8,128)}), f32[8,192,2,128]{3,1,2,0:T(8,128)}) %all-gather.3.cloned.1.call-update) | async-done | bytes 1572880 | tf_op jit(solution)/shard_map/all_gather | solution.py:10
  170.3 1.5 reduce_sum.25
  171.9 0.7 copy.6
  (56 shorter events, 11.0 us)
Async XLA Ops:
  6.5 163.8 %all-gather.3.cloned.1.call-start = ((), (), s32[]{:S(2)}) async-start(), calls=%async_computation | async-start | bytes 1966080 | tf_op jit(solution)/shard_map/all_gather | solution.py:10
  7.6 3.7 %collective-permute-start = (f32[2,192,2,128]{3,1,2,0:T(8,128)S(1)}, f32[2,192,2,128]{3,1,2,0:T(8,128)S(1)}, u32[]{:S(2)}, u32[]{:S(2)}) collective-permute-start(f32[2,192,2,128]{3,1,2,0:T(8,128)S(1)} %broadcast_select_fusion.7), channel_id=1, source_target_pairs={{0,1},{1,2},{2,3},{4,5},{5,6},{6,7},{8,9},{9,10},{10,11},{12,13},{... | collective-permute-start | bytes 1179656 | tf_op jit(solution)/shard_map/while/body/eval_jaxpr/ppermute | solution.py:31
  12.3 7.9 %collective-permute-start.1 = (f32[2,192,1,128]{3,1,2,0:T(8,128)S(1)}, f32[2,192,1,128]{3,1,2,0:T(8,128)S(1)}, u32[]{:S(2)}, u32[]{:S(2)}) collective-permute-start(f32[2,192,1,128]{3,1,2,0:T(8,128)S(1)} %get-tuple-element.385), channel_id=1, source_target_pairs={{4,0},{8,4},{12,8},{5,1},{9,5},{13,9},{6,2},{10,6},{14,10},{7,3},{... | collective-permute-start | bytes 589832 | tf_op jit(solution)/shard_map/while/body/eval_jaxpr/ppermute | solution.py:23
  13.6 8.1 %collective-permute-start.2 = (f32[2,192,1,128]{3,1,2,0:T(8,128)S(1)}, f32[2,192,1,128]{3,1,2,0:T(8,128)S(1)}, u32[]{:S(2)}, u32[]{:S(2)}) collective-permute-start(f32[2,192,1,128]{3,1,2,0:T(8,128)S(1)} %get-tuple-element.386), channel_id=1, source_target_pairs={{0,4},{4,8},{8,12},{1,5},{5,9},{9,13},{2,6},{6,10},{10,14},{3,7},{... | collective-permute-start | bytes 589832 | tf_op jit(solution)/shard_map/while/body/eval_jaxpr/ppermute | solution.py:20
  22.1 4.8 %copy-start = (f32[27,192,192]{2,1,0:T(8,128)S(1)}, f32[27,192,192]{2,1,0:T(8,128)}, u32[]{:S(2)}) copy-start(f32[27,192,192]{2,1,0:T(8,128)} %get-tuple-element.219) | copy-start | bytes 11943940 | tf_op jit(solution)/shard_map/while/body/eval_jaxpr/cond
  41.8 2.6 %collective-permute-start = (f32[2,192,2,128]{3,1,2,0:T(8,128)S(1)}, f32[2,192,2,128]{3,1,2,0:T(8,128)S(1)}, u32[]{:S(2)}, u32[]{:S(2)}) collective-permute-start(f32[2,192,2,128]{3,1,2,0:T(8,128)S(1)} %broadcast_select_fusion.7), channel_id=1, source_target_pairs={{0,1},{1,2},{2,3},{4,5},{5,6},{6,7},{8,9},{9,10},{10,11},{12,13},{... | collective-permute-start | bytes 1179656 | tf_op jit(solution)/shard_map/while/body/eval_jaxpr/ppermute | solution.py:31
  45.4 9.8 %collective-permute-start.1 = (f32[2,192,1,128]{3,1,2,0:T(8,128)S(1)}, f32[2,192,1,128]{3,1,2,0:T(8,128)S(1)}, u32[]{:S(2)}, u32[]{:S(2)}) collective-permute-start(f32[2,192,1,128]{3,1,2,0:T(8,128)S(1)} %get-tuple-element.385), channel_id=1, source_target_pairs={{4,0},{8,4},{12,8},{5,1},{9,5},{13,9},{6,2},{10,6},{14,10},{7,3},{... | collective-permute-start | bytes 589832 | tf_op jit(solution)/shard_map/while/body/eval_jaxpr/ppermute | solution.py:23
  46.7 9.7 %collective-permute-start.2 = (f32[2,192,1,128]{3,1,2,0:T(8,128)S(1)}, f32[2,192,1,128]{3,1,2,0:T(8,128)S(1)}, u32[]{:S(2)}, u32[]{:S(2)}) collective-permute-start(f32[2,192,1,128]{3,1,2,0:T(8,128)S(1)} %get-tuple-element.386), channel_id=1, source_target_pairs={{0,4},{4,8},{8,12},{1,5},{5,9},{9,13},{2,6},{6,10},{10,14},{3,7},{... | collective-permute-start | bytes 589832 | tf_op jit(solution)/shard_map/while/body/eval_jaxpr/ppermute | solution.py:20
  57.1 22.1 %collective-permute-start = (f32[2,192,2,128]{3,1,2,0:T(8,128)S(1)}, f32[2,192,2,128]{3,1,2,0:T(8,128)S(1)}, u32[]{:S(2)}, u32[]{:S(2)}) collective-permute-start(f32[2,192,2,128]{3,1,2,0:T(8,128)S(1)} %broadcast_select_fusion.7), channel_id=1, source_target_pairs={{0,1},{1,2},{2,3},{4,5},{5,6},{6,7},{8,9},{9,10},{10,11},{12,13},{... | collective-permute-start | bytes 1179656 | tf_op jit(solution)/shard_map/while/body/eval_jaxpr/ppermute | solution.py:31
  80.2 8.0 %collective-permute-start.1 = (f32[2,192,1,128]{3,1,2,0:T(8,128)S(1)}, f32[2,192,1,128]{3,1,2,0:T(8,128)S(1)}, u32[]{:S(2)}, u32[]{:S(2)}) collective-permute-start(f32[2,192,1,128]{3,1,2,0:T(8,128)S(1)} %get-tuple-element.385), channel_id=1, source_target_pairs={{4,0},{8,4},{12,8},{5,1},{9,5},{13,9},{6,2},{10,6},{14,10},{7,3},{... | collective-permute-start | bytes 589832 | tf_op jit(solution)/shard_map/while/body/eval_jaxpr/ppermute | solution.py:23
  81.5 8.2 %collective-permute-start.2 = (f32[2,192,1,128]{3,1,2,0:T(8,128)S(1)}, f32[2,192,1,128]{3,1,2,0:T(8,128)S(1)}, u32[]{:S(2)}, u32[]{:S(2)}) collective-permute-start(f32[2,192,1,128]{3,1,2,0:T(8,128)S(1)} %get-tuple-element.386), channel_id=1, source_target_pairs={{0,4},{4,8},{8,12},{1,5},{5,9},{9,13},{2,6},{6,10},{10,14},{3,7},{... | collective-permute-start | bytes 589832 | tf_op jit(solution)/shard_map/while/body/eval_jaxpr/ppermute | solution.py:20
  90.4 5.8 %collective-permute-start = (f32[2,192,2,128]{3,1,2,0:T(8,128)S(1)}, f32[2,192,2,128]{3,1,2,0:T(8,128)S(1)}, u32[]{:S(2)}, u32[]{:S(2)}) collective-permute-start(f32[2,192,2,128]{3,1,2,0:T(8,128)S(1)} %broadcast_select_fusion.7), channel_id=1, source_target_pairs={{0,1},{1,2},{2,3},{4,5},{5,6},{6,7},{8,9},{9,10},{10,11},{12,13},{... | collective-permute-start | bytes 1179656 | tf_op jit(solution)/shard_map/while/body/eval_jaxpr/ppermute | solution.py:31
  97.1 7.7 %collective-permute-start.1 = (f32[2,192,1,128]{3,1,2,0:T(8,128)S(1)}, f32[2,192,1,128]{3,1,2,0:T(8,128)S(1)}, u32[]{:S(2)}, u32[]{:S(2)}) collective-permute-start(f32[2,192,1,128]{3,1,2,0:T(8,128)S(1)} %get-tuple-element.385), channel_id=1, source_target_pairs={{4,0},{8,4},{12,8},{5,1},{9,5},{13,9},{6,2},{10,6},{14,10},{7,3},{... | collective-permute-start | bytes 589832 | tf_op jit(solution)/shard_map/while/body/eval_jaxpr/ppermute | solution.py:23
  98.4 7.9 %collective-permute-start.2 = (f32[2,192,1,128]{3,1,2,0:T(8,128)S(1)}, f32[2,192,1,128]{3,1,2,0:T(8,128)S(1)}, u32[]{:S(2)}, u32[]{:S(2)}) collective-permute-start(f32[2,192,1,128]{3,1,2,0:T(8,128)S(1)} %get-tuple-element.386), channel_id=1, source_target_pairs={{0,4},{4,8},{8,12},{1,5},{5,9},{9,13},{2,6},{6,10},{10,14},{3,7},{... | collective-permute-start | bytes 589832 | tf_op jit(solution)/shard_map/while/body/eval_jaxpr/ppermute | solution.py:20
Sparse Core Ops, SparseCore 0:
  107.9 62.3 all-gather.2
